TPU v7x, 32 devices: a whole 2x2x4 slice. The times are simulated.
32 devices in a mesh: grp: 4 (over z), leaf: 8 (over y, x, core).
Axes of the slice: x: 2, y: 2, z: 4, core: 2. Of those that a mesh axis runs over, the one named last changes fastest.
Arguments:
- basis_slab: bfloat16 [32768, 1024], P(('grp', 'leaf')), may hold values from -6 to 6
- live_counts: int32 [32], P(('grp', 'leaf')), may hold values from 128 to 1024, as said below
- pole_order: int32 [32, 1024], P(('grp', 'leaf')), may hold values from 0 to 1023, each once within a row
- leaf_diag: bfloat16 [32768, 1024], P(('grp', 'leaf')), may hold values from -0.1875 to 0.1875
- leaf_in: bfloat16 [32768, 128], P(('grp', 'leaf')), may hold values from -0.1875 to 0.1875
- leaf_out: bfloat16 [32768, 128], P(('grp', 'leaf')), may hold values from -0.5 to 0.5
- leaf_lift: bfloat16 [32, 128, 128], P(('grp', 'leaf')), may hold values from -0.375 to 0.375
- leaf_couple: bfloat16 [32, 128, 128], P(('grp', 'leaf')), may hold values from -0.5 to 0.5
- leaf_spread: bfloat16 [32, 128, 128], P(('grp', 'leaf')), may hold values from -0.4375 to 0.4375
- inner_lift: bfloat16 [28, 128, 128], replicated, may hold values from -0.375 to 0.375
- inner_couple: bfloat16 [30, 128, 128], replicated, may hold values from -0.5 to 0.5
- inner_spread: bfloat16 [28, 128, 128], replicated, may hold values from -0.4375 to 0.4375
Outputs:
- merged: bfloat16 [32768, 1024], P(('grp', 'leaf'))
Inputs may be any that keep to these rules, and one draw needn't show every extreme that they name: `live_counts`: each count is 1024, 512, 256 or 128, and some leaf has 1024. `pole_order`: each row names every slot's pole once.
All inputs are finite; a program needn't handle non-finite values.
Results may differ from a plain program's by a relative error of at most 0.0055.
Values may be sent and summed in bfloat16 or wider, within the bound.
A program may use at most 64 MiB of HBM per device.

v0:
```python
import jax
import jax.numpy as jnp
from jax import lax
from jax.sharding import PartitionSpec as P


def from_partner(block, axis, apart):
    count = lax.axis_size(axis)
    route = []
    for low in range(count):
        high = low | 1 << apart
        if high != low and high < count:
            route += [(low, high), (high, low)]
    return lax.ppermute(block, axis, route)


def transform(matrix, stacked):
    return jnp.dot(matrix.astype(jnp.float32), stacked, precision=lax.Precision.HIGHEST)


def local(
    basis_slab,
    live_counts,
    pole_order,
    leaf_diag,
    leaf_in,
    leaf_out,
    leaf_lift,
    leaf_couple,
    leaf_spread,
    inner_lift,
    inner_couple,
    inner_spread,
):
    groups = lax.axis_size("grp")
    leaves = lax.axis_size("leaf")
    devices = groups * leaves
    leaf_width = basis_slab.shape[0]
    slab_rows = basis_slab.shape[1]
    block_rows = leaf_width // devices
    levels = devices.bit_length() - 1
    leaf_bits = leaves.bit_length() - 1
    position = lax.axis_index("grp") * leaves + lax.axis_index("leaf")

    def redistribute(columns):
        arrived = lax.all_to_all(
            columns.reshape(devices, block_rows, slab_rows),
            ("grp", "leaf"),
            split_axis=0,
            concat_axis=0,
            tiled=True,
        )
        return arrived.reshape(leaf_width, slab_rows)

    def node_matrix(height, leaf_table, inner_table, offset):
        if height == 0:
            return leaf_table[0]
        own_node = jnp.right_shift(devices + position, height)
        return lax.dynamic_index_in_dim(inner_table, own_node - offset, 0, keepdims=False)

    leaf_rows = redistribute(basis_slab)
    slot_order = pole_order[0]
    live_count = live_counts[0]
    slots = jnp.take(leaf_rows, slot_order, axis=0)
    live_mask = jnp.arange(leaf_width, dtype=jnp.int32) < live_count
    masked = jnp.where(live_mask[:, None], slots, jnp.zeros_like(slots))
    skeleton = jnp.einsum("mk,mc->kc", leaf_in, masked, preferred_element_type=jnp.float32)
    crosses = []
    for height in range(leaf_bits):
        lifted = transform(node_matrix(height, leaf_lift, inner_lift, 4), skeleton)
        coupled = transform(node_matrix(height, leaf_couple, inner_couple, 2), skeleton)
        other_lift, other_cross = from_partner((lifted, coupled), "leaf", height)
        crosses.append(other_cross)
        skeleton = lifted + other_lift
    group_bits = groups.bit_length() - 1
    for height in range(leaf_bits, levels - 1):
        lifted = transform(node_matrix(height, leaf_lift, inner_lift, 4), skeleton)
        coupled = transform(node_matrix(height, leaf_couple, inner_couple, 2), skeleton)
        other_lift, other_cross = (
            from_partner(lifted.astype(jnp.bfloat16), "grp", height - leaf_bits).astype(
                lifted.dtype
            ),
            from_partner(coupled.astype(jnp.bfloat16), "grp", height - leaf_bits).astype(
                coupled.dtype
            ),
        )
        crosses.append(other_cross)
        skeleton = lifted + other_lift
    coupled = transform(node_matrix(levels - 1, leaf_couple, inner_couple, 2), skeleton)
    crosses.append(
        from_partner(coupled.astype(jnp.bfloat16), "grp", group_bits - 1).astype(coupled.dtype)
    )
    incoming = crosses[levels - 1]
    for height in range(levels - 2, -1, -1):
        incoming = (
            transform(node_matrix(height, leaf_spread, inner_spread, 4), incoming) + crosses[height]
        )
    incoming_b = incoming.astype(jnp.bfloat16)
    tile_rows = leaf_width // 8
    tile_count = live_count // tile_rows

    def one_tile(tile_index, merged_rows):
        row_start = tile_index * tile_rows
        diag_rows = lax.dynamic_slice_in_dim(leaf_diag, row_start, tile_rows, 0)
        out_rows = lax.dynamic_slice_in_dim(leaf_out, row_start, tile_rows, 0)
        value = jnp.dot(diag_rows, masked, preferred_element_type=jnp.float32) + jnp.dot(
            out_rows, incoming_b, preferred_element_type=jnp.float32
        )
        return lax.dynamic_update_slice_in_dim(merged_rows, value, row_start, 0)

    merged_rows = lax.fori_loop(
        0, tile_count, one_tile, jnp.zeros((leaf_width, slab_rows), jnp.float32)
    )
    updated = jnp.where(live_mask[:, None], merged_rows, slots.astype(jnp.float32)).astype(
        jnp.bfloat16
    )
    inverse = (
        jnp.zeros((leaf_width,), jnp.int32)
        .at[slot_order]
        .set(jnp.arange(leaf_width, dtype=jnp.int32))
    )
    restored = jnp.take(updated, inverse, axis=0)
    return redistribute(restored)


def solution(mesh):
    placed = (
        P(("grp", "leaf"), None),
        P(("grp", "leaf")),
        P(("grp", "leaf"), None),
        P(("grp", "leaf"), None),
        P(("grp", "leaf"), None),
        P(("grp", "leaf"), None),
        P(("grp", "leaf"), None, None),
        P(("grp", "leaf"), None, None),
        P(("grp", "leaf"), None, None),
        P(),
        P(),
        P(),
    )
    return jax.shard_map(
        local, mesh=mesh, in_specs=placed, out_specs=P(("grp", "leaf"), None), check_vma=False
    )
```

profile of v0, /device:TPU:0, one launch (start us, length us, event | category | flops | bytes accessed | tf_op | source)
XLA Modules:
  0.0 219.5 jit_solution(8093613755789859259)
XLA Ops:
  0.0 7.3 %all-to-all-start = ((bf16[32,32,1024]{2,1,0:T(8,128)(2,1)}), bf16[32,32,1024]{2,1,0:T(8,128)(2,1)S(1)}, u32[]{:S(2)}, u32[]{:S(2)}) async-start(bf16[32,32,1024]{2,1,0:T(8,128)(2,1)} %bitcast.81), calls=%async_computation | async-start | bytes 4194304 | tf_op jit(solution)/shard_map/all_to_all | solution.py:46
  8.0 48.0 %all-to-all-done = bf16[32,32,1024]{2,1,0:T(8,128)(2,1)S(1)} async-done(((bf16[32,32,1024]{2,1,0:T(8,128)(2,1)}), bf16[32,32,1024]{2,1,0:T(8,128)(2,1)S(1)}, u32[]{:S(2)}, u32[]{:S(2)}) %all-to-all-start) | async-done | bytes 2097184 | tf_op jit(solution)/shard_map/all_to_all | solution.py:46
  56.1 5.4 %gather_fusion = bf16[1024,1024]{1,0:T(8,128)(2,1)} fusion(bf16[1024,1024]{1,0:T(8,128)(2,1)S(1)} %bitcast.78, s32[1024]{0:T(1024)S(1)} %fusion.46), kind=kCustom, calls=%fused_computation.clone | custom fusion | bytes 4198400 | tf_op jit(solution)/shard_map/jit(_take)/gather | solution.py:64
  61.4 2.1 broadcast_select_fusion.2
  66.3 2.2 %collective-permute-done = f32[128,1024]{0,1:T(8,128)} collective-permute-done((f32[128,1024]{0,1:T(8,128)}, f32[128,1024]{0,1:T(8,128)}, u32[]{:S(2)}, u32[]{:S(2)}) %collective-permute-start) | collective-permute-done | bytes 524320 | tf_op jit(solution)/shard_map/ppermute | solution.py:14
  68.6 2.4 %fusion.20 = f32[128,1024]{1,0:T(8,128)} fusion(f32[128,1024]{0,1:T(8,128)} %convolution_bitcast_fusion.2, f32[128,1024]{0,1:T(8,128)} %collective-permute-done, bf16[28,128,128]{2,1,0:T(8,128)(2,1)} %param.25, s32[]{:T(128)S(6)} %select_n.63), kind=kOutput, calls=%fused_computation.35 | convolution fusion | flops 201457664 | bytes 1605636 | tf_op jit(solution)/shard_map/dot_general | solution.py:18
  71.0 1.6 collective-permute-start.1
  72.6 12.7 %collective-permute-done.1 = f32[128,1024]{1,0:T(8,128)} collective-permute-done((f32[128,1024]{1,0:T(8,128)}, f32[128,1024]{1,0:T(8,128)}, u32[]{:S(2)}, u32[]{:S(2)}) %collective-permute-start.1) | collective-permute-done | bytes 524320 | tf_op jit(solution)/shard_map/ppermute | solution.py:14
  85.3 2.4 %fusion.16 = f32[128,1024]{1,0:T(8,128)} fusion(f32[128,1024]{1,0:T(8,128)} %fusion.20, f32[128,1024]{1,0:T(8,128)} %collective-permute-done.1, bf16[28,128,128]{2,1,0:T(8,128)(2,1)} %param.25, s32[]{:T(128)S(6)} %select_n.64), kind=kOutput, calls=%fused_computation.31 | convolution fusion | flops 201457664 | bytes 1605636 | tf_op jit(solution)/shard_map/dot_general | solution.py:18
  87.7 1.4 collective-permute-start.2
  89.2 4.3 %scatter_custom_fusion = s32[1024]{0:T(1024)S(1)} fusion(s32[1024]{0:T(1024)S(1)} %bitcast.84, s32[1024]{0:T(1024)S(1)} %iota.9, s32[]{:T(128)} %constant.84.clone.1), kind=kCustom, calls=%fused_computation.79 | custom fusion | bytes 4100 | tf_op jit(solution)/shard_map/scatter | solution.py:120
  93.5 7.6 %collective-permute-done.2 = f32[128,1024]{1,0:T(8,128)} collective-permute-done((f32[128,1024]{1,0:T(8,128)}, f32[128,1024]{1,0:T(8,128)}, u32[]{:S(2)}, u32[]{:S(2)}) %collective-permute-start.2) | collective-permute-done | bytes 524320 | tf_op jit(solution)/shard_map/ppermute | solution.py:14
  101.2 1.6 fusion.60
  103.4 1.6 fusion.18
  105.0 1.6 collective-permute-start.7
  106.7 1.6 convolution_convert_fusion
  108.3 1.6 collective-permute-start.5
  110.4 1.8 collective-permute-start.4
  112.2 1.6 fusion.14
  115.0 4.8 %collective-permute-done.5 = bf16[128,1024]{1,0:T(8,128)(2,1)S(1)} collective-permute-done((bf16[128,1024]{1,0:T(8,128)(2,1)S(1)}, bf16[128,1024]{1,0:T(8,128)(2,1)S(1)}, u32[]{:S(2)}, u32[]{:S(2)}) %collective-permute-start.5) | collective-permute-done | bytes 262176 | tf_op jit(solution)/shard_map/ppermute | solution.py:14
  119.8 2.9 %collective-permute-done.4 = bf16[128,1024]{1,0:T(8,128)(2,1)S(1)} collective-permute-done((bf16[128,1024]{1,0:T(8,128)(2,1)S(1)}, bf16[128,1024]{1,0:T(8,128)(2,1)S(1)}, u32[]{:S(2)}, u32[]{:S(2)}) %collective-permute-start.4) | collective-permute-done | bytes 262176 | tf_op jit(solution)/shard_map/ppermute | solution.py:14
  125.0 1.2 convolution_add_fusion.2
  126.2 1.3 fusion.7
  128.6 1.6 broadcast_in_dim.33
  130.1 3.1 %while.10 = (s32[]{:T(128)}, bf16[1024,1024]{1,0:T(8,128)(2,1)}, s32[]{:T(128)}, bf16[1024,1024]{1,0:T(8,128)(2,1)}, bf16[1024,1024]{1,0:T(8,128)(2,1)S(1)}, /*i...) while((s32[]{:T(128)}, bf16[1024,1024]{1,0:T(8,128)(2,1)}, ...), condition=%wide.region_1.3_spmd, body=%wide.region_0.0_spmd.sunk | while | flops 302120960 | bytes 4228255 | solution.py:111
  130.1 1.4 fusion.81
  131.5 1.7 fusion.82
  133.2 2.7 %select_convert_fusion = bf16[1024,1024]{1,0:T(8,128)(2,1)S(1)} fusion(bf16[1024,1024]{1,0:T(8,128)(2,1)} %get-tuple-element.44, pred[1024]{0:T(1024)(128)(4,1)S(1)} %get-tuple-element.75, bf16[1024,1024]{1,0:T(8,128)(2,1)} %gather_fusion, pred[1024]{0:T(1024)(128)(4,1)S(1)} %get-tuple-element.76), kind=kLoop, calls=%fused_computation.10 | loop fusion | flops 3145728 | bytes 6293504 | tf_op jit(solution)/shard_map/convert_element_type | solution.py:114
  136.0 5.3 %gather_fusion.1 = bf16[1024,1024]{1,0:T(8,128)(2,1)} fusion(bf16[1024,1024]{1,0:T(8,128)(2,1)S(1)} %select_convert_fusion, s32[1024]{0:T(1024)S(1)} %fusion.47), kind=kCustom, calls=%fused_computation.1.clone | custom fusion | bytes 4198400 | tf_op jit(solution)/shard_map/jit(_take)/gather | solution.py:122
  141.3 1.9 broadcast_select_fusion
  143.2 75.0 %all_to_all.10 = bf16[32,32,1024]{2,1,0:T(8,128)(2,1)S(1)} all-to-all(bf16[32,32,1024]{2,1,0:T(8,128)(2,1)S(1)} %bitcast.79), channel_id=1, replica_groups=mesh['grp'=4,'leaf'=8] {'grp','leaf'}, dimensions={0} | all-to-all | bytes 4194304 | tf_op jit(solution)/shard_map/all_to_all | solution.py:46
  218.2 1.3 copy.24
  (37 shorter events, 8.2 us)
Async XLA Ops:
  0.0 103.4 %copy-start = (bf16[30,128,128]{2,1,0:T(8,128)(2,1)S(1)}, bf16[30,128,128]{2,1,0:T(8,128)(2,1)}, u32[]{:S(2)}) copy-start(bf16[30,128,128]{2,1,0:T(8,128)(2,1)} %param.26) | copy-start | bytes 2949124
  0.0 8.0 %copy-start.4 = (s32[1,1024]{1,0:T(1,128)S(1)}, s32[1,1024]{1,0:T(1,128)}, u32[]{:S(2)}) copy-start(s32[1,1024]{1,0:T(1,128)} %param.18) | copy-start | bytes 12292
  0.0 56.1 %all-to-all-start = ((bf16[32,32,1024]{2,1,0:T(8,128)(2,1)}), bf16[32,32,1024]{2,1,0:T(8,128)(2,1)S(1)}, u32[]{:S(2)}, u32[]{:S(2)}) async-start(bf16[32,32,1024]{2,1,0:T(8,128)(2,1)} %bitcast.81), calls=%async_computation | async-start | bytes 4194304 | tf_op jit(solution)/shard_map/all_to_all | solution.py:46
  61.4 2.2 copy-start.3
  63.6 1.6 copy-start.5
  64.4 0.8 copy-start.1
  66.3 2.3 %collective-permute-start = (f32[128,1024]{0,1:T(8,128)}, f32[128,1024]{0,1:T(8,128)}, u32[]{:S(2)}, u32[]{:S(2)}) collective-permute-start(f32[128,1024]{0,1:T(8,128)} %convolution_bitcast_fusion.2), channel_id=1, source_target_pairs={{0,1},{1,0},{2,3},{3,2},{4,5},{5,4},{6,7},{7,6},{8,9},{9,8},{10,11... | collective-permute-start | bytes 1572872 | tf_op jit(solution)/shard_map/ppermute | solution.py:14
  71.0 14.3 %collective-permute-start.1 = (f32[128,1024]{1,0:T(8,128)}, f32[128,1024]{1,0:T(8,128)}, u32[]{:S(2)}, u32[]{:S(2)}) collective-permute-start(f32[128,1024]{1,0:T(8,128)} %fusion.20), channel_id=1, source_target_pairs={{0,2},{2,0},{1,3},{3,1},{4,6},{6,4},{5,7},{7,5},{8,10},{10,8},{9,1... | collective-permute-start | bytes 1572872 | tf_op jit(solution)/shard_map/ppermute | solution.py:14
  87.7 13.4 %collective-permute-start.2 = (f32[128,1024]{1,0:T(8,128)}, f32[128,1024]{1,0:T(8,128)}, u32[]{:S(2)}, u32[]{:S(2)}) collective-permute-start(f32[128,1024]{1,0:T(8,128)} %fusion.16), channel_id=1, source_target_pairs={{0,4},{4,0},{1,5},{5,1},{2,6},{6,2},{3,7},{7,3},{8,12},{12,8},{9,1... | collective-permute-start | bytes 1572872 | tf_op jit(solution)/shard_map/ppermute | solution.py:14
  102.8 7.2 %collective-permute-start.3 = (bf16[128,1024]{1,0:T(8,128)(2,1)S(1)}, bf16[128,1024]{1,0:T(8,128)(2,1)S(1)}, u32[]{:S(2)}, u32[]{:S(2)}) collective-permute-start(bf16[128,1024]{1,0:T(8,128)(2,1)S(1)} %get-tuple-element.73), channel_id=1, source_target_pairs={{0,8},{8,0},{16,24},{24,16},{1,9},{9,1},{17,25},{25,17},{2,10},{10... | collective-permute-start | bytes 786440 | tf_op jit(solution)/shard_map/ppermute | solution.py:14
  105.0 9.5 %copy-start.2 = (f32[1024,128]{1,0:T(8,128)S(1)}, f32[1024,128]{1,0:T(8,128)}, u32[]{:S(2)}) copy-start(f32[1024,128]{1,0:T(8,128)} %copy-done.1) | copy-start | bytes 1572868
  105.0 9.5 %copy-start.6 = (bf16[1,128,128]{2,1,0:T(8,128)(2,1)S(1)}, bf16[1,128,128]{2,1,0:T(8,128)(2,1)}, u32[]{:S(2)}) copy-start(bf16[1,128,128]{2,1,0:T(8,128)(2,1)} %param.23) | copy-start | bytes 98308
  105.0 19.9 %collective-permute-start.7 = (f32[128,1024]{1,0:T(8,128)S(1)}, f32[128,1024]{1,0:T(8,128)S(1)}, u32[]{:S(2)}, u32[]{:S(2)}) collective-permute-start(f32[128,1024]{1,0:T(8,128)S(1)} %fusion.18), channel_id=1, source_target_pairs={{0,2},{2,0},{1,3},{3,1},{4,6},{6,4},{5,7},{7,5},{8,10},{10,8},{9,1... | collective-permute-start | bytes 1572872 | tf_op jit(solution)/shard_map/ppermute | solution.py:14
  108.3 11.6 %collective-permute-start.5 = (bf16[128,1024]{1,0:T(8,128)(2,1)S(1)}, bf16[128,1024]{1,0:T(8,128)(2,1)S(1)}, u32[]{:S(2)}, u32[]{:S(2)}) collective-permute-start(bf16[128,1024]{1,0:T(8,128)(2,1)S(1)} %convolution_convert_fusion), channel_id=1, source_target_pairs={{0,8},{8,0},{16,24},{24,16},{1,9},{9,1},{17,25},{25,17},{2,10},{10... | collective-permute-start | bytes 786440 | tf_op jit(solution)/shard_map/ppermute | solution.py:14
  110.4 12.4 %collective-permute-start.4 = (bf16[128,1024]{1,0:T(8,128)(2,1)S(1)}, bf16[128,1024]{1,0:T(8,128)(2,1)S(1)}, u32[]{:S(2)}, u32[]{:S(2)}) collective-permute-start(bf16[128,1024]{1,0:T(8,128)(2,1)S(1)} %convolution_convert_fusion.1), channel_id=1, source_target_pairs={{0,16},{16,0},{8,24},{24,8},{1,17},{17,1},{9,25},{25,9},{2,18},{18... | collective-permute-start | bytes 786440 | tf_op jit(solution)/shard_map/ppermute | solution.py:14
  113.8 11.1 %collective-permute-start.6 = (f32[128,1024]{1,0:T(8,128)S(1)}, f32[128,1024]{1,0:T(8,128)S(1)}, u32[]{:S(2)}, u32[]{:S(2)}) collective-permute-start(f32[128,1024]{1,0:T(8,128)S(1)} %fusion.14), channel_id=1, source_target_pairs={{0,4},{4,0},{1,5},{5,1},{2,6},{6,2},{3,7},{7,3},{8,12},{12,8},{9,1... | collective-permute-start | bytes 1572872 | tf_op jit(solution)/shard_map/ppermute | solution.py:14
  114.9 11.3 %copy-start.7 = (bf16[1,128,128]{2,1,0:T(8,128)(2,1)S(1)}, bf16[1,128,128]{2,1,0:T(8,128)(2,1)}, u32[]{:S(2)}) copy-start(bf16[1,128,128]{2,1,0:T(8,128)(2,1)} %param.24) | copy-start | bytes 98308
  114.9 11.2 %collective-permute-start.8 = (f32[128,1024]{0,1:T(8,128)S(1)}, f32[128,1024]{0,1:T(8,128)S(1)}, u32[]{:S(2)}, u32[]{:S(2)}) collective-permute-start(f32[128,1024]{0,1:T(8,128)S(1)} %convolution_bitcast_fusion), channel_id=1, source_target_pairs={{0,1},{1,0},{2,3},{3,2},{4,5},{5,4},{6,7},{7,6},{8,9},{9,8},{10,11... | collective-permute-start | bytes 1572872 | tf_op jit(solution)/shard_map/ppermute | solution.py:14
where the time goes:
time: 221 us; the launch traced here: 219 us
  waiting for transfers between devices  78.5 us (36%)
  blocking collectives  75 us (34%)
  matrix products  21.8 us (10%)
  local copies, waits for them, and re-layouts  19.8 us (9%)
  starting transfers between devices  16.7 us (8%)
  other arithmetic  6.75 us (3%)
    all_to_all x1, blocking collectives, redistribute(): lax.all_to_all(columns.reshape(devices, block_rows, slab_rows), ('grp', '...  75 us
    all_to_all x1, waiting for transfers between devices, redistribute(): lax.all_to_all(columns.reshape(devices, block_rows, slab_rows), ('grp', '...  48 us
    ppermute x9, waiting for transfers between devices, from_partner(): return lax.ppermute(block, axis, route)  30.5 us
    dot_general x13, matrix products, transform(): jnp.dot(matrix.astype(jnp.float32), stacked, precision=lax.Precision.HIGH...  17.9 us
    ppermute x9, starting transfers between devices, from_partner(): return lax.ppermute(block, axis, route)  9.37 us
    all_to_all x1, starting transfers between devices, redistribute(): lax.all_to_all(columns.reshape(devices, block_rows, slab_rows), ('grp', '...  7.33 us
    gather x1, local copies, waits for them, and re-layouts, local(): slots = jnp.take(leaf_rows, slot_order, axis=0)  5.36 us
    gather x1, local copies, waits for them, and re-layouts, local(): restored = jnp.take(updated, inverse, axis=0)  5.34 us
  transfers between devices with their start and end apart: 10, of which 7 were waited for; matrix products, arithmetic and copies ran while one was open for 6% of the time, Pallas kernels for 0%

commit v1 on v0

--- a/solution.py
+++ b/solution.py
@@ -1,7 +1,323 @@
+import functools
+
 import jax
 import jax.numpy as jnp
 from jax import lax
+from jax.experimental import pallas as pl
+from jax.experimental.pallas import tpu as pltpu
 from jax.sharding import PartitionSpec as P
+
+MESH = pl.DeviceIdType.MESH
+CHUNKS = 4
+AHEAD = 2
+STRIDE = 3
+
+
+def row_dot(a, b):
+    return jnp.dot(a, b, preferred_element_type=jnp.float32)
+
+
+def fine_dot(matrix, value):
+    high = value.astype(jnp.bfloat16)
+    low = (value - high.astype(jnp.float32)).astype(jnp.bfloat16)
+    return row_dot(matrix, high) + row_dot(matrix, low)
+
+
+def fused_kernel(
+    groups,
+    leaves,
+    slab,
+    live,
+    order,
+    diag,
+    gen_in,
+    gen_out,
+    leaf_lift,
+    leaf_couple,
+    leaf_spread,
+    inner_lift,
+    inner_couple,
+    inner_spread,
+    out,
+    arrived,
+    staged,
+    select,
+    diag_poles,
+    in_poles,
+    out_poles,
+    leaf_sent,
+    leaf_got,
+    sent,
+    got,
+    cross,
+    own,
+    in_send,
+    in_recv,
+    out_send,
+    out_recv,
+    tree_send,
+    tree_recv,
+    local_sem,
+):
+    devices = groups * leaves
+    levels = devices.bit_length() - 1
+    chunks, width, cols = arrived.shape
+    block = width // devices
+    me = lax.axis_index("grp") * leaves + lax.axis_index("leaf")
+
+    def place(device):
+        return (lax.div(device, leaves), lax.rem(device, leaves))
+
+    def node(height):
+        return lax.div(devices + me, 1 << height)
+
+    def sibling(index):
+        return index + 1 - 2 * lax.rem(index, 2)
+
+    def partner(height):
+        bit = lax.rem(lax.div(me, 1 << height), 2)
+        return place(me + (1 - 2 * bit) * (1 << height))
+
+    def others(step):
+        def body(shift, carry):
+            step(lax.rem(me + shift, devices))
+            return carry
+
+        lax.fori_loop(1, devices, body, 0)
+
+    def rows_of(device):
+        return pl.ds(pl.multiple_of(device * block, block), block)
+
+    def cols_of(chunk):
+        return pl.ds(chunk * cols, cols)
+
+    barrier = pltpu.get_barrier_semaphore()
+    others(
+        lambda device: pl.semaphore_signal(
+            barrier, inc=1, device_id=place(device), device_id_type=MESH
+        )
+    )
+    pl.semaphore_wait(barrier, devices - 1)
+
+    def send_in(chunk):
+        others(
+            lambda device: pltpu.make_async_remote_copy(
+                src_ref=slab.at[rows_of(device), cols_of(chunk)],
+                dst_ref=arrived.at[chunk, rows_of(me)],
+                send_sem=in_send.at[chunk],
+                recv_sem=in_recv.at[chunk],
+                device_id=place(device),
+                device_id_type=MESH,
+            ).start()
+        )
+        pltpu.make_async_copy(
+            slab.at[rows_of(me), cols_of(chunk)],
+            arrived.at[chunk, rows_of(me)],
+            local_sem.at[0, chunk],
+        ).start()
+
+    def send_out(chunk):
+        others(
+            lambda device: pltpu.make_async_remote_copy(
+                src_ref=staged.at[chunk, rows_of(device)],
+                dst_ref=out.at[rows_of(me), cols_of(chunk)],
+                send_sem=out_send.at[chunk],
+                recv_sem=out_recv.at[chunk],
+                device_id=place(device),
+                device_id_type=MESH,
+            ).start()
+        )
+        pltpu.make_async_copy(
+            staged.at[chunk, rows_of(me)],
+            out.at[rows_of(me), cols_of(chunk)],
+            local_sem.at[1, chunk],
+        ).start()
+
+    def wait_all(buffer, semaphore):
+        most = buffer.at[pl.ds(0, width - block)]
+        pltpu.make_async_copy(most, most, semaphore).wait()
+
+    def wait_own(buffer, semaphore):
+        part = buffer.at[pl.ds(0, block)]
+        pltpu.make_async_copy(part, part, semaphore).wait()
+
+    def tree_copy(chunk, height):
+        source, target = (
+            (leaf_sent.at[chunk], leaf_got.at[chunk])
+            if height == 0
+            else (sent.at[chunk, height - 1], got.at[chunk, height - 1])
+        )
+        return pltpu.make_async_remote_copy(
+            src_ref=source,
+            dst_ref=target,
+            send_sem=tree_send.at[chunk, height],
+            recv_sem=tree_recv.at[chunk, height],
+            device_id=partner(height),
+            device_id_type=MESH,
+        )
+
+    for chunk in range(min(AHEAD, chunks)):
+        send_in(chunk)
+
+    slot = lax.broadcasted_iota(jnp.int32, (1, width), 1)
+    key = jnp.where(slot < live[...], order[...], -1)
+    part = min(256, width)
+    for start in range(0, width, part):
+        pole = lax.broadcasted_iota(jnp.int32, (part, width), 0) + start
+        select[start : start + part, :] = jnp.where(pole == key, 1.0, 0.0).astype(jnp.bfloat16)
+
+    def fold(index, carry):
+        start = pl.multiple_of(index * part, part)
+        rows = pl.ds(start, part)
+        chosen = select[rows, :]
+        half = row_dot(chosen, diag[...]).astype(jnp.bfloat16)
+        full = lax.dot_general(
+            half, select[...], (((1,), (1,)), ((), ())), preferred_element_type=jnp.float32
+        )
+        alive = jnp.sum(chosen.astype(jnp.float32), axis=1, keepdims=True)
+        pole = lax.broadcasted_iota(jnp.int32, (part, width), 0) + start
+        same = jnp.where(pole == lax.broadcasted_iota(jnp.int32, (part, width), 1), 1.0, 0.0)
+        diag_poles[rows, :] = (full + (1.0 - alive) * same).astype(jnp.bfloat16)
+        out_poles[rows, :] = row_dot(chosen, gen_out[...]).astype(jnp.bfloat16)
+        in_poles[rows, :] = row_dot(chosen, gen_in[...])
+        return carry
+
+    lax.fori_loop(0, width // part, fold, 0)
+    gather = in_poles[...].T.astype(jnp.bfloat16)
+
+    def first(chunk):
+        wait_all(arrived.at[chunk], in_recv.at[chunk])
+        wait_own(arrived.at[chunk], local_sem.at[0, chunk])
+        skeleton = row_dot(gather, arrived[chunk])
+        lifted = fine_dot(leaf_lift[0], skeleton)
+        own[chunk] = lifted
+        leaf_sent[chunk, 0] = lifted.astype(jnp.bfloat16)
+        leaf_sent[chunk, 1] = fine_dot(leaf_couple[0], skeleton).astype(jnp.bfloat16)
+        tree_copy(chunk, 0).start()
+
+    def rise(chunk, height):
+        tree_copy(chunk, height).wait()
+        if height == 0:
+            cross[chunk, 0] = leaf_got[chunk, 1].astype(jnp.float32)
+            skeleton = own[chunk] + leaf_got[chunk, 0].astype(jnp.float32)
+        else:
+            mine = node(height)
+            other = sibling(mine)
+            theirs = got[chunk, height - 1]
+            cross[chunk, height] = row_dot(inner_couple[other - 2], theirs)
+            if height == levels - 1:
+                return
+            skeleton = fine_dot(inner_lift[mine - 4], own[chunk]) + row_dot(
+                inner_lift[other - 4], theirs
+            )
+        own[chunk] = skeleton
+        sent[chunk, height] = skeleton.astype(jnp.bfloat16)
+        tree_copy(chunk, height + 1).start()
+
+    def finish(chunk):
+        incoming = cross[chunk, levels - 1]
+        for height in range(levels - 2, -1, -1):
+            spread = leaf_spread[0] if height == 0 else inner_spread[node(height) - 4]
+            incoming = fine_dot(spread, incoming) + cross[chunk, height]
+        incoming = incoming.astype(jnp.bfloat16)
+
+        def rows_done(index, carry):
+            rows = pl.ds(pl.multiple_of(index * part, part), part)
+            value = row_dot(diag_poles[rows, :], arrived[chunk]) + row_dot(
+                out_poles[rows, :], incoming
+            )
+            staged[chunk, rows, :] = value.astype(jnp.bfloat16)
+            return carry
+
+        lax.fori_loop(0, width // part, rows_done, 0)
+        send_out(chunk)
+
+    for tick in range(STRIDE * (chunks - 1) + levels + 1):
+        for chunk in range(chunks):
+            stage = tick - STRIDE * chunk
+            if stage == 0:
+                first(chunk)
+                if chunk + AHEAD < chunks:
+                    send_in(chunk + AHEAD)
+            elif 1 <= stage <= levels:
+                rise(chunk, stage - 1)
+                if stage == levels:
+                    finish(chunk)
+
+    for chunk in range(chunks):
+        wait_all(arrived.at[chunk], in_send.at[chunk])
+        wait_all(staged.at[chunk], out_send.at[chunk])
+        wait_all(staged.at[chunk], out_recv.at[chunk])
+        wait_own(staged.at[chunk], local_sem.at[1, chunk])
+
+
+def fused(
+    basis_slab,
+    live_counts,
+    pole_order,
+    leaf_diag,
+    leaf_in,
+    leaf_out,
+    leaf_lift,
+    leaf_couple,
+    leaf_spread,
+    inner_lift,
+    inner_couple,
+    inner_spread,
+):
+    groups = lax.axis_size("grp")
+    leaves = lax.axis_size("leaf")
+    devices = groups * leaves
+    levels = devices.bit_length() - 1
+    width, slab_rows = basis_slab.shape
+    rank = leaf_in.shape[1]
+    cols = slab_rows // CHUNKS
+    vmem = pl.BlockSpec(memory_space=pltpu.VMEM)
+    anywhere = pl.BlockSpec(memory_space=pl.ANY)
+    half = jnp.bfloat16
+    return pl.pallas_call(
+        functools.partial(fused_kernel, groups, leaves),
+        out_shape=jax.ShapeDtypeStruct((width, slab_rows), half),
+        in_specs=[anywhere] + [vmem] * 11,
+        out_specs=anywhere,
+        scratch_shapes=[
+            pltpu.VMEM((CHUNKS, width, cols), half),
+            pltpu.VMEM((CHUNKS, width, cols), half),
+            pltpu.VMEM((width, width), half),
+            pltpu.VMEM((width, width), half),
+            pltpu.VMEM((width, rank), jnp.float32),
+            pltpu.VMEM((width, rank), half),
+            pltpu.VMEM((CHUNKS, 2, rank, cols), half),
+            pltpu.VMEM((CHUNKS, 2, rank, cols), half),
+            pltpu.VMEM((CHUNKS, levels - 1, rank, cols), half),
+            pltpu.VMEM((CHUNKS, levels - 1, rank, cols), half),
+            pltpu.VMEM((CHUNKS, levels, rank, cols), jnp.float32),
+            pltpu.VMEM((CHUNKS, rank, cols), jnp.float32),
+            pltpu.SemaphoreType.DMA((CHUNKS,)),
+            pltpu.SemaphoreType.DMA((CHUNKS,)),
+            pltpu.SemaphoreType.DMA((CHUNKS,)),
+            pltpu.SemaphoreType.DMA((CHUNKS,)),
+            pltpu.SemaphoreType.DMA((CHUNKS, levels)),
+            pltpu.SemaphoreType.DMA((CHUNKS, levels)),
+            pltpu.SemaphoreType.DMA((2, CHUNKS)),
+        ],
+        compiler_params=pltpu.CompilerParams(
+            collective_id=0, has_side_effects=True, vmem_limit_bytes=56 * 1024 * 1024
+        ),
+    )(
+        basis_slab,
+        live_counts.reshape(1, 1),
+        pole_order,
+        leaf_diag,
+        leaf_in,
+        leaf_out,
+        leaf_lift,
+        leaf_couple,
+        leaf_spread,
+        inner_lift,
+        inner_couple,
+        inner_spread,
+    )
 
 
 def from_partner(block, axis, apart):
@@ -138,6 +454,13 @@
         P(),
         P(),
     )
+
+    def step(basis_slab, *rest):
+        devices = mesh.shape["grp"] * mesh.shape["leaf"]
+        block_rows = basis_slab.shape[0] // devices
+        whole_tiles = block_rows % 16 == 0 and basis_slab.shape[1] % (128 * CHUNKS) == 0
+        return (fused if whole_tiles else local)(basis_slab, *rest)
+
     return jax.shard_map(
-        local, mesh=mesh, in_specs=placed, out_specs=P(("grp", "leaf"), None), check_vma=False
-    )
+        step, mesh=mesh, in_specs=placed, out_specs=P(("grp", "leaf"), None), check_vma=False
+    )

time: 221 us -> 126 us (0.57)
  the two profiles are of different devices: /device:TPU:0 before, /device:TPU:13 now
where the time goes in v1:
time: 126 us
  Pallas kernels  122 us (97%)
  local copies, waits for them, and re-layouts  3.08 us (2%)
    pallas_call x1, Pallas kernels, fused(): pl.pallas_call(functools.partial(fused_kernel, groups, leaves), out_shape...  122 us
    unnamed x1, local copies, waits for them, and re-layouts  3.08 us

profile of v1, /device:TPU:13, one launch (start us, length us, event | category | flops | bytes accessed | tf_op | source)
XLA Modules:
  0.0 126.1 jit_solution(11210082438877854146)
XLA Ops:
  0.7 122.4 %shard_map.118 = bf16[1024,1024]{1,0:T(8,128)(2,1)} custom-call(bf16[1024,1024]{1,0:T(8,128)(2,1)} %slab.1, s32[1,1]{1,0:T(1,128)} %bitcast.1.live, s32[1,1024]{1,0:T(1,128)} %order.1, bf16[1024,1024]{1,0:T(8,128)(2,1)} %diag.1, bf16[1024,128]{1,0:T(8,128)(2,1)} %gen_in.1, bf16[1024,128]{1,0:T(8,128)(2,1)} %gen_out.1, bf16[1,128,128]{2,1,0:T(8,128)(2,1)} %leaf_lift.1, ...), custom_call_target="tpu_custom_call" | custom-call | tf_op jit(solution)/shard_map/pallas_call | solution.py:278
  123.0 3.1 %copy.15 = bf16[1024,1024]{1,0:T(8,128)(2,1)} copy(bf16[1024,1024]{1,0:T(8,128)(2,1)} %shard_map.118) | data formatting | bytes 4194304

commit v2 on v1

--- a/solution.py
+++ b/solution.py
@@ -10,17 +10,23 @@
 MESH = pl.DeviceIdType.MESH
 CHUNKS = 4
 AHEAD = 2
-STRIDE = 3
+STRIDE = 1
 
 
 def row_dot(a, b):
     return jnp.dot(a, b, preferred_element_type=jnp.float32)
 
 
-def fine_dot(matrix, value):
-    high = value.astype(jnp.bfloat16)
-    low = (value - high.astype(jnp.float32)).astype(jnp.bfloat16)
-    return row_dot(matrix, high) + row_dot(matrix, low)
+def times(matrix, rows):
+    return lax.dot_general(
+        rows, matrix, (((1,), (1,)), ((), ())), preferred_element_type=jnp.float32
+    )
+
+
+def fine_times(matrix, rows):
+    high = rows.astype(jnp.bfloat16)
+    low = (rows - high.astype(jnp.float32)).astype(jnp.bfloat16)
+    return times(matrix, high) + times(matrix, low)
 
 
 def fused_kernel(
@@ -41,16 +47,23 @@
     out,
     arrived,
     staged,
+    diag_here,
+    in_here,
+    out_here,
+    lifts,
+    couples,
+    spreads,
+    leaf_tables,
     select,
     diag_poles,
     in_poles,
     out_poles,
-    leaf_sent,
-    leaf_got,
-    sent,
-    got,
+    up_sent,
+    up_got,
+    top,
     cross,
-    own,
+    down_sent,
+    down_got,
     in_send,
     in_recv,
     out_send,
@@ -58,12 +71,17 @@
     tree_send,
     tree_recv,
     local_sem,
+    load_sem,
+    table_send,
+    table_recv,
 ):
     devices = groups * leaves
-    levels = devices.bit_length() - 1
     chunks, width, cols = arrived.shape
     block = width // devices
-    me = lax.axis_index("grp") * leaves + lax.axis_index("leaf")
+    part_cols = cols // leaves
+    group = lax.axis_index("grp")
+    seat = lax.axis_index("leaf")
+    me = group * leaves + seat
 
     def place(device):
         return (lax.div(device, leaves), lax.rem(device, leaves))
@@ -74,9 +92,12 @@
     def sibling(index):
         return index + 1 - 2 * lax.rem(index, 2)
 
-    def partner(height):
-        bit = lax.rem(lax.div(me, 1 << height), 2)
-        return place(me + (1 - 2 * bit) * (1 << height))
+    def seats(step):
+        def body(shift, carry):
+            step(lax.rem(seat + shift, leaves))
+            return carry
+
+        lax.fori_loop(1, leaves, body, 0)
 
     def others(step):
         def body(shift, carry):
@@ -141,23 +162,41 @@
         part = buffer.at[pl.ds(0, block)]
         pltpu.make_async_copy(part, part, semaphore).wait()
 
-    def tree_copy(chunk, height):
-        source, target = (
-            (leaf_sent.at[chunk], leaf_got.at[chunk])
-            if height == 0
-            else (sent.at[chunk, height - 1], got.at[chunk, height - 1])
-        )
+    def tree_copy(source, target, chunk, stage, device):
         return pltpu.make_async_remote_copy(
             src_ref=source,
             dst_ref=target,
-            send_sem=tree_send.at[chunk, height],
-            recv_sem=tree_recv.at[chunk, height],
-            device_id=partner(height),
+            send_sem=tree_send.at[stage, chunk],
+            recv_sem=tree_recv.at[stage, chunk],
+            device_id=device,
             device_id_type=MESH,
+        )
+
+    own_tables = (leaf_lift, leaf_couple, leaf_spread)
+    for index, table in enumerate(own_tables):
+        seats(
+            lambda other: pltpu.make_async_remote_copy(
+                src_ref=table.at[0],
+                dst_ref=leaf_tables.at[seat, index],
+                send_sem=table_send.at[0],
+                recv_sem=table_recv.at[0],
+                device_id=(group, other),
+                device_id_type=MESH,
+            ).start()
         )
 
     for chunk in range(min(AHEAD, chunks)):
         send_in(chunk)
+
+    pairs = [(diag, diag_here), (gen_in, in_here), (gen_out, out_here)]
+    pairs += [(inner_lift, lifts), (inner_couple, couples), (inner_spread, spreads)]
+    pairs += [(table.at[0], leaf_tables.at[seat, index]) for index, table in enumerate(own_tables)]
+    loads = [
+        pltpu.make_async_copy(source, target, load_sem.at[index])
+        for index, (source, target) in enumerate(pairs)
+    ]
+    for load in loads:
+        load.start()
 
     slot = lax.broadcasted_iota(jnp.int32, (1, width), 1)
     key = jnp.where(slot < live[...], order[...], -1)
@@ -166,11 +205,14 @@
         pole = lax.broadcasted_iota(jnp.int32, (part, width), 0) + start
         select[start : start + part, :] = jnp.where(pole == key, 1.0, 0.0).astype(jnp.bfloat16)
 
+    for load in loads:
+        load.wait()
+
     def fold(index, carry):
         start = pl.multiple_of(index * part, part)
         rows = pl.ds(start, part)
         chosen = select[rows, :]
-        half = row_dot(chosen, diag[...]).astype(jnp.bfloat16)
+        half = row_dot(chosen, diag_here[...]).astype(jnp.bfloat16)
         full = lax.dot_general(
             half, select[...], (((1,), (1,)), ((), ())), preferred_element_type=jnp.float32
         )
@@ -178,48 +220,115 @@
         pole = lax.broadcasted_iota(jnp.int32, (part, width), 0) + start
         same = jnp.where(pole == lax.broadcasted_iota(jnp.int32, (part, width), 1), 1.0, 0.0)
         diag_poles[rows, :] = (full + (1.0 - alive) * same).astype(jnp.bfloat16)
-        out_poles[rows, :] = row_dot(chosen, gen_out[...]).astype(jnp.bfloat16)
-        in_poles[rows, :] = row_dot(chosen, gen_in[...])
+        out_poles[rows, :] = row_dot(chosen, out_here[...]).astype(jnp.bfloat16)
+        in_poles[rows, :] = row_dot(chosen, in_here[...])
         return carry
 
     lax.fori_loop(0, width // part, fold, 0)
     gather = in_poles[...].T.astype(jnp.bfloat16)
+
+    few = leaf_tables.at[pl.ds(0, leaves - 1)]
+    pltpu.make_async_copy(few, few, table_recv.at[0]).wait()
+
+    def seat_rows(other):
+        return pl.ds(pl.multiple_of(other * part_cols, part_cols), part_cols)
+
+    def wait_up(chunk, semaphore):
+        most = up_got.at[chunk, pl.ds(0, leaves - 1)]
+        pltpu.make_async_copy(most, most, semaphore).wait()
+
+    def wait_top(chunk, semaphore):
+        most = top.at[chunk, pl.ds(0, groups - 1)]
+        pltpu.make_async_copy(most, most, semaphore).wait()
+
+    def wait_down(chunk, semaphore):
+        most = down_got.at[chunk, pl.ds(0, cols - part_cols)]
+        pltpu.make_async_copy(most, most, semaphore).wait()
+
+    def node(local):
+        depth = local.bit_length() - 1
+        return (groups + group) * (1 << depth) + (local - (1 << depth))
+
+    def lift_of(local):
+        return leaf_tables[local - leaves, 0] if local >= leaves else lifts[node(local) - 4]
+
+    def couple_of(local):
+        return leaf_tables[local - leaves, 1] if local >= leaves else couples[node(local) - 2]
+
+    def spread_of(local):
+        return leaf_tables[local - leaves, 2] if local >= leaves else spreads[node(local) - 4]
 
     def first(chunk):
         wait_all(arrived.at[chunk], in_recv.at[chunk])
         wait_own(arrived.at[chunk], local_sem.at[0, chunk])
-        skeleton = row_dot(gather, arrived[chunk])
-        lifted = fine_dot(leaf_lift[0], skeleton)
-        own[chunk] = lifted
-        leaf_sent[chunk, 0] = lifted.astype(jnp.bfloat16)
-        leaf_sent[chunk, 1] = fine_dot(leaf_couple[0], skeleton).astype(jnp.bfloat16)
-        tree_copy(chunk, 0).start()
-
-    def rise(chunk, height):
-        tree_copy(chunk, height).wait()
-        if height == 0:
-            cross[chunk, 0] = leaf_got[chunk, 1].astype(jnp.float32)
-            skeleton = own[chunk] + leaf_got[chunk, 0].astype(jnp.float32)
-        else:
-            mine = node(height)
-            other = sibling(mine)
-            theirs = got[chunk, height - 1]
-            cross[chunk, height] = row_dot(inner_couple[other - 2], theirs)
-            if height == levels - 1:
-                return
-            skeleton = fine_dot(inner_lift[mine - 4], own[chunk]) + row_dot(
-                inner_lift[other - 4], theirs
+        up_sent[chunk] = row_dot(gather, arrived[chunk]).T.astype(jnp.bfloat16)
+        seats(
+            lambda other: tree_copy(
+                up_sent.at[chunk, seat_rows(other)], up_got.at[chunk, seat], chunk, 0, (group, other)
+            ).start()
+        )
+        up_got[chunk, seat] = up_sent[chunk, seat_rows(seat), :]
+
+    def second(chunk):
+        wait_up(chunk, tree_recv.at[0, chunk])
+        skeletons = {leaves + index: up_got[chunk, index] for index in range(leaves)}
+        for local in range(2 * leaves - 1, 1, -1):
+            cross[chunk, local ^ 1] = times(couple_of(local), skeletons[local])
+            if local % 2 == 0:
+                skeletons[local // 2] = (
+                    times(lift_of(local), skeletons[local])
+                    + times(lift_of(local + 1), skeletons[local + 1])
+                ).astype(jnp.bfloat16)
+        top[chunk, groups + group] = skeletons[1]
+
+        def body(shift, carry):
+            tree_copy(
+                top.at[chunk, groups + group],
+                top.at[chunk, groups + group],
+                chunk,
+                1,
+                (lax.rem(group + shift, groups), seat),
+            ).start()
+            return carry
+
+        lax.fori_loop(1, groups, body, 0)
+
+    def third(chunk):
+        wait_top(chunk, tree_recv.at[1, chunk])
+        for index in range(groups - 1, 1, -1):
+            top[chunk, index] = (
+                times(lifts[2 * index - 4], top[chunk, 2 * index])
+                + times(lifts[2 * index - 3], top[chunk, 2 * index + 1])
+            ).astype(jnp.bfloat16)
+        incoming = None
+        for height in range(groups.bit_length() - 2, -1, -1):
+            mine = lax.div(groups + group, 1 << height)
+            other = mine + 1 - 2 * lax.rem(mine, 2)
+            crossed = times(couples[other - 2], top[chunk, other])
+            if incoming is not None:
+                crossed = crossed + fine_times(spreads[mine - 4], incoming)
+            incoming = crossed
+        passed = {1: incoming}
+        for local in range(2, 2 * leaves):
+            passed[local] = (
+                fine_times(spread_of(local), passed[local // 2]) + cross[chunk, local]
             )
-        own[chunk] = skeleton
-        sent[chunk, height] = skeleton.astype(jnp.bfloat16)
-        tree_copy(chunk, height + 1).start()
+        for index in range(leaves):
+            down_sent[chunk, index] = passed[leaves + index].astype(jnp.bfloat16)
+        seats(
+            lambda other: tree_copy(
+                down_sent.at[chunk, other],
+                down_got.at[chunk, seat_rows(seat)],
+                chunk,
+                2,
+                (group, other),
+            ).start()
+        )
+        down_got[chunk, seat_rows(seat), :] = down_sent[chunk, seat]
 
     def finish(chunk):
-        incoming = cross[chunk, levels - 1]
-        for height in range(levels - 2, -1, -1):
-            spread = leaf_spread[0] if height == 0 else inner_spread[node(height) - 4]
-            incoming = fine_dot(spread, incoming) + cross[chunk, height]
-        incoming = incoming.astype(jnp.bfloat16)
+        wait_down(chunk, tree_recv.at[2, chunk])
+        incoming = down_got[chunk].astype(jnp.float32).T.astype(jnp.bfloat16)
 
         def rows_done(index, carry):
             rows = pl.ds(pl.multiple_of(index * part, part), part)
@@ -232,20 +341,21 @@
         lax.fori_loop(0, width // part, rows_done, 0)
         send_out(chunk)
 
-    for tick in range(STRIDE * (chunks - 1) + levels + 1):
+    stages = (first, second, third, finish)
+    for tick in range(STRIDE * (chunks - 1) + len(stages)):
         for chunk in range(chunks):
             stage = tick - STRIDE * chunk
-            if stage == 0:
-                first(chunk)
-                if chunk + AHEAD < chunks:
+            if 0 <= stage < len(stages):
+                stages[stage](chunk)
+                if stage == 0 and chunk + AHEAD < chunks:
                     send_in(chunk + AHEAD)
-            elif 1 <= stage <= levels:
-                rise(chunk, stage - 1)
-                if stage == levels:
-                    finish(chunk)
-
+
+    pltpu.make_async_copy(few, few, table_send.at[0]).wait()
     for chunk in range(chunks):
         wait_all(arrived.at[chunk], in_send.at[chunk])
+        wait_up(chunk, tree_send.at[0, chunk])
+        wait_top(chunk, tree_send.at[1, chunk])
+        wait_down(chunk, tree_send.at[2, chunk])
         wait_all(staged.at[chunk], out_send.at[chunk])
         wait_all(staged.at[chunk], out_recv.at[chunk])
         wait_own(staged.at[chunk], local_sem.at[1, chunk])
@@ -278,28 +388,38 @@
     return pl.pallas_call(
         functools.partial(fused_kernel, groups, leaves),
         out_shape=jax.ShapeDtypeStruct((width, slab_rows), half),
-        in_specs=[anywhere] + [vmem] * 11,
+        in_specs=[anywhere] + [vmem] * 2 + [anywhere] * 9,
         out_specs=anywhere,
         scratch_shapes=[
             pltpu.VMEM((CHUNKS, width, cols), half),
             pltpu.VMEM((CHUNKS, width, cols), half),
             pltpu.VMEM((width, width), half),
+            pltpu.VMEM((width, rank), half),
+            pltpu.VMEM((width, rank), half),
+            pltpu.VMEM(inner_lift.shape, half),
+            pltpu.VMEM(inner_couple.shape, half),
+            pltpu.VMEM(inner_spread.shape, half),
+            pltpu.VMEM((leaves, 3, rank, rank), half),
+            pltpu.VMEM((width, width), half),
             pltpu.VMEM((width, width), half),
             pltpu.VMEM((width, rank), jnp.float32),
             pltpu.VMEM((width, rank), half),
-            pltpu.VMEM((CHUNKS, 2, rank, cols), half),
-            pltpu.VMEM((CHUNKS, 2, rank, cols), half),
-            pltpu.VMEM((CHUNKS, levels - 1, rank, cols), half),
-            pltpu.VMEM((CHUNKS, levels - 1, rank, cols), half),
-            pltpu.VMEM((CHUNKS, levels, rank, cols), jnp.float32),
-            pltpu.VMEM((CHUNKS, rank, cols), jnp.float32),
+            pltpu.VMEM((CHUNKS, cols, rank), half),
+            pltpu.VMEM((CHUNKS, leaves, cols // leaves, rank), half),
+            pltpu.VMEM((CHUNKS, 2 * groups, cols // leaves, rank), half),
+            pltpu.VMEM((CHUNKS, 2 * leaves, cols // leaves, rank), jnp.float32),
+            pltpu.VMEM((CHUNKS, leaves, cols // leaves, rank), half),
+            pltpu.VMEM((CHUNKS, cols, rank), half),
             pltpu.SemaphoreType.DMA((CHUNKS,)),
             pltpu.SemaphoreType.DMA((CHUNKS,)),
             pltpu.SemaphoreType.DMA((CHUNKS,)),
             pltpu.SemaphoreType.DMA((CHUNKS,)),
-            pltpu.SemaphoreType.DMA((CHUNKS, levels)),
-            pltpu.SemaphoreType.DMA((CHUNKS, levels)),
+            pltpu.SemaphoreType.DMA((3, CHUNKS)),
+            pltpu.SemaphoreType.DMA((3, CHUNKS)),
             pltpu.SemaphoreType.DMA((2, CHUNKS)),
+            pltpu.SemaphoreType.DMA((9,)),
+            pltpu.SemaphoreType.DMA((1,)),
+            pltpu.SemaphoreType.DMA((1,)),
         ],
         compiler_params=pltpu.CompilerParams(
             collective_id=0, has_side_effects=True, vmem_limit_bytes=56 * 1024 * 1024
@@ -458,7 +578,7 @@
     def step(basis_slab, *rest):
         devices = mesh.shape["grp"] * mesh.shape["leaf"]
         block_rows = basis_slab.shape[0] // devices
-        whole_tiles = block_rows % 16 == 0 and basis_slab.shape[1] % (128 * CHUNKS) == 0
+        whole_tiles = block_rows % 16 == 0 and basis_slab.shape[1] % (128 * CHUNKS) == 0 and basis_slab.shape[1] % (16 * CHUNKS * mesh.shape["leaf"]) == 0
         return (fused if whole_tiles else local)(basis_slab, *rest)
 
     return jax.shard_map(

time: 126 us -> 109 us (0.87)
  Pallas kernels: 122 us -> 105 us
    pallas_call x1, Pallas kernels: 122 us -> 105 us  [fused(): pl.pallas_call(functools.partial(fused_kernel, groups, leaves), out_shape...]
where the time goes in v2:
time: 109 us
  Pallas kernels  105 us (96%)
  local copies, waits for them, and re-layouts  3.08 us (3%)
    pallas_call x1, Pallas kernels, fused(): pl.pallas_call(functools.partial(fused_kernel, groups, leaves), out_shape...  105 us
    unnamed x1, local copies, waits for them, and re-layouts  3.08 us

profile of v2, /device:TPU:13, one launch (start us, length us, event | category | flops | bytes accessed | tf_op | source)
XLA Modules:
  0.0 108.7 jit_solution(445915347045551486)
XLA Ops:
  0.7 104.9 %shard_map.118 = bf16[1024,1024]{1,0:T(8,128)(2,1)} custom-call(bf16[1024,1024]{1,0:T(8,128)(2,1)} %slab.1, s32[1,1]{1,0:T(1,128)} %bitcast.1.live, s32[1,1024]{1,0:T(1,128)} %order.1, bf16[1024,1024]{1,0:T(8,128)(2,1)} %diag.1, bf16[1024,128]{1,0:T(8,128)(2,1)} %gen_in.1, bf16[1024,128]{1,0:T(8,128)(2,1)} %gen_out.1, bf16[1,128,128]{2,1,0:T(8,128)(2,1)} %leaf_lift.1, ...), custom_call_target="tpu_custom_call" | custom-call | tf_op jit(solution)/shard_map/pallas_call | solution.py:388
  105.6 3.1 %copy.15 = bf16[1024,1024]{1,0:T(8,128)(2,1)} copy(bf16[1024,1024]{1,0:T(8,128)(2,1)} %shard_map.118) | data formatting | bytes 4194304

commit v3 on v2

--- a/solution.py
+++ b/solution.py
@@ -347,7 +347,7 @@
             stage = tick - STRIDE * chunk
             if 0 <= stage < len(stages):
                 stages[stage](chunk)
-                if stage == 0 and chunk + AHEAD < chunks:
+                if stage == 1 and chunk + AHEAD < chunks:
                     send_in(chunk + AHEAD)
 
     pltpu.make_async_copy(few, few, table_send.at[0]).wait()

time: 109 us -> 109 us (level)
  no operation moved by 1% of the time
where the time goes in v3:
time: 109 us
  Pallas kernels  105 us (96%)
  local copies, waits for them, and re-layouts  3.08 us (3%)
    pallas_call x1, Pallas kernels, fused(): pl.pallas_call(functools.partial(fused_kernel, groups, leaves), out_shape...  105 us
    unnamed x1, local copies, waits for them, and re-layouts  3.08 us

profile of v3, /device:TPU:13, one launch (start us, length us, event | category | flops | bytes accessed | tf_op | source)
XLA Modules:
  0.0 108.6 jit_solution(5394352002288559592)
XLA Ops:
  0.7 104.8 %shard_map.118 = bf16[1024,1024]{1,0:T(8,128)(2,1)} custom-call(bf16[1024,1024]{1,0:T(8,128)(2,1)} %slab.1, s32[1,1]{1,0:T(1,128)} %bitcast.1.live, s32[1,1024]{1,0:T(1,128)} %order.1, bf16[1024,1024]{1,0:T(8,128)(2,1)} %diag.1, bf16[1024,128]{1,0:T(8,128)(2,1)} %gen_in.1, bf16[1024,128]{1,0:T(8,128)(2,1)} %gen_out.1, bf16[1,128,128]{2,1,0:T(8,128)(2,1)} %leaf_lift.1, ...), custom_call_target="tpu_custom_call" | custom-call | tf_op jit(solution)/shard_map/pallas_call | solution.py:388
  105.5 3.1 %copy.15 = bf16[1024,1024]{1,0:T(8,128)(2,1)} copy(bf16[1024,1024]{1,0:T(8,128)(2,1)} %shard_map.118) | data formatting | bytes 4194304
